TPU v7x, 512 devices: a whole 4x8x8 slice. The times are simulated.
512 devices in a mesh: row: 128 (over y, z, core), col: 4 (over x).
Axes of the slice: x: 4, y: 8, z: 8, core: 2. Of those that a mesh axis runs over, the one named last changes fastest.
Arguments:
- feat_in: bfloat16 [4096, 256, 256], P('row', 'col'), may hold values from -6 to 6
- conv_weight: bfloat16 [2304, 256], P('col'), may hold values from -0.125 to 0.125
- conv_bias: float32 [256], replicated, may hold values from -4 to 4
- proj_weight: bfloat16 [256, 768], replicated, may hold values from -0.375 to 0.375
- qkv_weight: bfloat16 [768, 2304], P('row'), may hold values from -2 to 2
- tissue: int32 [2048, 128], P('row', 'col'), may hold values from 0 to 1, as said below
- phase: int32 [2048, 128], P('row', 'col'), may hold values from 0 to 3, as said below
Outputs:
- attended: bfloat16 [2048, 128, 768], P('row', 'col')
Inputs may be any that keep to these rules, and one draw needn't show every extreme that they name: Within each column strip, phase is the token column plus an offset drawn for each token row, modulo 4. In each device's block of tokens, every phase holds at least one tissue token.
All inputs are finite; a program needn't handle non-finite values.
Results may differ from a plain program's by a relative error of at most 0.0065.
Values may be sent and summed in bfloat16 or wider, within the bound.
A program may use at most 64 MiB of HBM per device.

v0:
```python
import jax
import jax.numpy as jnp
from jax import lax
from jax.sharding import PartitionSpec as P

HD = 64
DILATION_STEP = 4


def partner(array, axis, apart):
    return lax.ppermute(array, axis, [(i, i ^ 1 << apart) for i in range(lax.axis_size(axis))])


def shifted(array, axis, by):
    length = lax.axis_size(axis)
    pairs = [(i, i + by) for i in range(length) if 0 <= i + by < length]
    return lax.ppermute(array, axis, pairs)


def layer_norm(values):
    centred = values - jnp.mean(values, axis=-1, keepdims=True)
    spread_rows = jnp.mean(centred * centred, axis=-1, keepdims=True)
    return centred * lax.rsqrt(spread_rows + 1e-05)


def fold_rows(operand, piece):
    return jnp.dot(operand, piece, preferred_element_type=jnp.float32)


def split_pair(buffer, bit, mine):
    slots = buffer.shape[0]
    view = buffer.reshape((slots >> bit + 1, 2, 1 << bit) + buffer.shape[1:])
    keep = jnp.where(mine == 0, view[:, 0], view[:, 1])
    send = jnp.where(mine == 0, view[:, 1], view[:, 0])
    return (keep, send)


def join_pair(keep, got, mine, shape):
    first = jnp.where(mine == 0, keep, got)
    second = jnp.where(mine == 0, got, keep)
    return jnp.stack([first, second], axis=1).reshape(shape)


def route_sender(payload, flags):
    mine_index = lax.axis_index("row")
    for bit in range(flag_bits(flags)):
        mine = mine_index >> bit & 1
        keep_a, send_a = split_pair(payload, bit, mine)
        keep_b, send_b = split_pair(flags, bit, mine)
        got_a, got_b = partner((send_a, send_b), "row", bit)
        payload = join_pair(keep_a, got_a, mine, payload.shape)
        flags = join_pair(keep_b, got_b, mine, flags.shape)
    return (payload, flags)


def route_back(payload):
    mine_index = lax.axis_index("row")
    for bit in range(flag_bits(payload)):
        mine = mine_index >> bit & 1
        keep_a, send_a = split_pair(payload, bit, mine)
        got_a = partner(send_a, "row", bit)
        payload = join_pair(keep_a, got_a, mine, payload.shape)
    return payload


def flag_bits(buffer):
    return buffer.shape[0].bit_length() - 1


def attend(queries, keys_all, values_all, key_live, query_live):
    row_count = queries.shape[0]
    model_width = queries.shape[1]
    head_count = model_width // HD
    query_heads = queries.reshape(row_count, head_count, HD).transpose(1, 0, 2)
    key_heads = keys_all.reshape(keys_all.shape[0], head_count, HD).transpose(1, 0, 2)
    value_heads = values_all.reshape(values_all.shape[0], head_count, HD).transpose(1, 0, 2)
    allowed = (key_live > 0.5)[None, :]

    def one_head(operands):
        query_head, key_head, value_head = operands
        scores = jnp.einsum(
            "qd,kd->qk", query_head, key_head, preferred_element_type=jnp.float32
        ) * HD ** (-0.5)
        scores = jnp.where(allowed, scores, -1e30)
        top_score = jnp.max(scores, axis=1, keepdims=True)
        weights = jnp.where(allowed, jnp.exp(scores - top_score), 0.0)
        denominator = jnp.sum(weights, axis=1, keepdims=True)
        return (
            jnp.dot(weights.astype(jnp.bfloat16), value_head, preferred_element_type=jnp.float32)
            / denominator
        )

    stacked = lax.map(one_head, (query_heads, key_heads, value_heads))
    merged = stacked.transpose(1, 0, 2).reshape(row_count, model_width)
    return (merged * query_live.astype(jnp.float32)[:, None]).astype(jnp.bfloat16)


def local(feat_in, conv_weight, conv_bias, proj_weight, qkv_weight, tissue, phase):
    in_rows, in_cols, channels = feat_in.shape
    out_rows = in_rows // 2
    out_cols = in_cols // 2
    token_count = out_rows * out_cols
    band_count = lax.axis_size("row")
    owner_labels = 2 * DILATION_STEP
    capacity = token_count // owner_labels
    model_width = qkv_weight.shape[0] * band_count
    left_edge = shifted(feat_in[:, in_cols - 1 :, :], "col", 1)
    widened = jnp.concatenate([left_edge, feat_in], axis=1)
    upper_edge = shifted(widened[in_rows - 1 :], "row", 1)
    padded = jnp.concatenate([upper_edge, widened], axis=0)
    windows = []
    for row_tap in range(3):
        for col_tap in range(3):
            window = padded[
                row_tap : row_tap + in_rows - 1 : 2, col_tap : col_tap + in_cols - 1 : 2, :
            ]
            windows.append(window.reshape(token_count, channels))
    patches = jnp.concatenate(windows, axis=1)
    conv_sum = fold_rows(patches, lax.all_gather(conv_weight, "col", axis=0, tiled=True))
    features = jax.nn.gelu(conv_sum + conv_bias).astype(jnp.bfloat16)
    tokens_bf = layer_norm(
        jnp.dot(features, proj_weight, preferred_element_type=jnp.float32)
    ).astype(jnp.bfloat16)
    phase_labels = phase.reshape(token_count)
    indicator_matrix = (
        phase_labels[:, None] == jnp.arange(DILATION_STEP, dtype=jnp.int32)[None, :]
    ).astype(jnp.int32)
    ranking = jnp.sum(
        (jnp.cumsum(indicator_matrix, axis=0) - indicator_matrix) * indicator_matrix, axis=1
    )
    target = (2 * phase_labels + ranking // capacity) * capacity + ranking % capacity
    inverse = (
        jnp.zeros((token_count,), jnp.int32)
        .at[target]
        .set(jnp.arange(token_count, dtype=jnp.int32))
    )
    tissue_flag = tissue.reshape(token_count).astype(jnp.bfloat16)
    flag_out = tissue_flag[inverse].reshape(owner_labels, capacity)
    qkv_local = fold_rows(tokens_bf, lax.all_gather(qkv_weight, "row", axis=0, tiled=True)).astype(
        jnp.bfloat16
    )
    arrived, arrived_flag = route_sender(
        qkv_local[inverse].reshape(owner_labels, capacity, 3 * model_width), flag_out
    )
    arrived_qkv = arrived.reshape(token_count, 3 * model_width)
    query_flag = arrived_flag.reshape(token_count)
    keys_values = arrived_qkv[:, model_width:]
    partner_kv, partner_flag = partner((keys_values, query_flag), "row", 0)
    joined_kv = jnp.concatenate([keys_values, partner_kv], axis=0)
    key_flag = jnp.concatenate([query_flag, partner_flag], axis=0)
    attended_rows = attend(
        arrived_qkv[:, :model_width],
        joined_kv[:, :model_width],
        joined_kv[:, model_width:],
        key_flag,
        query_flag,
    )
    returned = route_back(attended_rows.reshape(owner_labels, capacity, model_width))
    outputs = returned.reshape(token_count, model_width)[target]
    return outputs.reshape(out_rows, out_cols, model_width)


def solution(mesh):
    in_specs = (
        P("row", "col", None),
        P("col", None),
        P(),
        P(),
        P("row", None),
        P("row", "col"),
        P("row", "col"),
    )
    out_specs = P("row", "col", None)
    return jax.shard_map(local, mesh=mesh, in_specs=in_specs, out_specs=out_specs, check_vma=False)
```

profile of v0, /device:TPU:1, one launch (start us, length us, event | category | flops | bytes accessed | tf_op | source)
XLA Modules:
  0.0 378.8 jit_solution(9001759087257412841)
XLA Ops:
  9.0 3.9 %collective-permute-start.4 = (bf16[32,1,256]{2,1,0:T(2,128)(2,1)S(1)}, bf16[32,1,256]{2,1,0:T(2,128)(2,1)S(1)}, u32[]{:S(2)}, u32[]{:S(2)}) collective-permute-start(bf16[32,1,256]{2,1,0:T(2,128)(2,1)S(1)} %slice.131), channel_id=1, source_target_pairs={{0,1},{1,2},{2,3},{4,5},{5,6},{6,7},{8,9},{9,10},{10,11},{12,13},{... | collective-permute-start | bytes 49160 | tf_op jit(solution)/shard_map/ppermute | solution.py:17
  17.0 2.4 scatter_custom_fusion
  19.5 8.8 %slice.137 = bf16[16,32,256]{2,1,0:T(8,128)(2,1)} slice(bf16[32,64,256]{2,1,0:T(8,128)(2,1)} %param.9), slice={[0:31:2], [0:63:2], [0:256:1]} | slice | bytes 524288 | tf_op jit(solution)/shard_map/slice | solution.py:114
  28.2 7.0 %slice.138 = bf16[16,32,256]{2,1,0:T(8,128)(2,1)S(1)} slice(bf16[32,64,256]{2,1,0:T(8,128)(2,1)} %param.9), slice={[0:31:2], [1:64:2], [0:256:1]} | slice | bytes 524288 | tf_op jit(solution)/shard_map/slice | solution.py:114
  36.9 4.8 %collective-permute-start.5 = (bf16[1,65,256]{2,1,0:T(8,128)(2,1)S(1)}, bf16[1,65,256]{2,1,0:T(8,128)(2,1)S(1)}, u32[]{:S(2)}, u32[]{:S(2)}) collective-permute-start(bf16[1,65,256]{2,1,0:T(8,128)(2,1)S(1)} %fusion.51), channel_id=1, source_target_pairs={{0,4},{4,8},{8,12},{12,16},{16,20},{20,24},{24,28},{28,32},{32,36}... | collective-permute-start | bytes 99848 | tf_op jit(solution)/shard_map/ppermute | solution.py:17
  42.4 5.0 %slice.136 = bf16[16,32,256]{2,1,0:T(8,128)(2,1)} slice(bf16[32,65,256]{2,1,0:T(8,128)(2,1)S(1)} %pad_maximum_fusion.2), slice={[0:31:2], [0:63:2], [0:256:1]} | slice | bytes 524288 | tf_op jit(solution)/shard_map/slice | solution.py:114
  47.5 5.0 %slice.139 = bf16[16,32,256]{2,1,0:T(8,128)(2,1)} slice(bf16[32,65,256]{2,1,0:T(8,128)(2,1)S(1)} %pad_maximum_fusion.2), slice={[1:32:2], [0:63:2], [0:256:1]} | slice | bytes 524288 | tf_op jit(solution)/shard_map/slice | solution.py:114
  53.2 5.1 %slice.133 = bf16[16,32,256]{2,1,0:T(8,128)(2,1)} slice(bf16[33,65,256]{2,1,0:T(8,128)(2,1)S(1)} %maximum_maximum_fusion), slice={[0:31:2], [0:63:2], [0:256:1]} | slice | bytes 524288 | tf_op jit(solution)/shard_map/slice | solution.py:114
  58.3 5.0 %slice.134 = bf16[16,32,256]{2,1,0:T(8,128)(2,1)} slice(bf16[33,65,256]{2,1,0:T(8,128)(2,1)S(1)} %maximum_maximum_fusion), slice={[0:31:2], [1:64:2], [0:256:1]} | slice | bytes 524288 | tf_op jit(solution)/shard_map/slice | solution.py:114
  72.8 3.5 fusion.67
  76.6 57.6 %all-gather.6.cloned.1.call-done = bf16[128,6,2304]{2,1,0:T(8,128)(2,1)} async-done(((bf16[1,6,2304]{2,1,0:T(8,128)(2,1)}), bf16[128,6,2304]{2,1,0:T(8,128)(2,1)}) %all-gather.6.cloned.1.call-update) | async-done | bytes 3538960 | tf_op jit(solution)/shard_map/all_gather | solution.py:139
  134.2 6.6 %reshape.571 = bf16[768,2304]{1,0:T(8,128)(2,1)} reshape(bf16[128,6,2304]{2,1,0:T(8,128)(2,1)} %all-gather.6.cloned.1.call-done) | data formatting | bytes 7077888
  140.9 4.5 %convolution_convert_fusion = bf16[512,2304]{1,0:T(8,128)(2,1)S(1)} fusion(bf16[768,2304]{1,0:T(8,128)(2,1)} %reshape.571, f32[512,768]{1,0:T(8,128)} %copy-done.4, f32[512]{0:T(512)S(1)} %add_rsqrt_fusion, f32[512]{0:T(512)S(1)} %broadcast_multiply_fusion.1), kind=kOutput, calls=%fused_computation.28 | convolution fusion | flops 1814298624 | bytes 7475200 | tf_op jit(solution)/shard_map/dot_general | solution.py:27
  145.4 3.4 gather_fusion.1
  148.8 2.9 fusion.23
  153.9 2.9 collective-permute-done.6
  162.0 27.2 %collective-permute-done.7 = bf16[2,2,64,2304]{3,2,1,0:T(8,128)(2,1)} collective-permute-done((bf16[2,2,64,2304]{3,2,1,0:T(8,128)(2,1)}, bf16[2,2,64,2304]{3,2,1,0:T(8,128)(2,1)}, u32[]{:S(2)}, u32[]{:S(2)}) %collective-permute-start.7) | collective-permute-done | bytes 1179680 | tf_op jit(solution)/shard_map/ppermute | solution.py:11
  192.1 3.3 collective-permute-start.8
  195.5 3.5 gather_fusion
  199.1 49.2 %collective-permute-done.8 = bf16[1,4,64,2304]{3,2,1,0:T(8,128)(2,1)} collective-permute-done((bf16[1,4,64,2304]{3,2,1,0:T(8,128)(2,1)}, bf16[1,4,64,2304]{3,2,1,0:T(8,128)(2,1)}, u32[]{:S(2)}, u32[]{:S(2)}) %collective-permute-start.8) | collective-permute-done | bytes 1179680 | tf_op jit(solution)/shard_map/ppermute | solution.py:11
  251.3 2.5 collective-permute-start.9
  258.8 2.4 collective-permute-done.1
  261.2 3.0 collective-permute-start.2
  266.6 4.7 %collective-permute-start.3 = (bf16[512]{0:T(512)(128)(2,1)S(1)}, bf16[512]{0:T(512)(128)(2,1)S(1)}, u32[]{:S(2)}, u32[]{:S(2)}) collective-permute-start(bf16[512]{0:T(512)(128)(2,1)S(1)} %reshape_reshape.30), channel_id=1, source_target_pairs={{0,4},{4,0},{8,12},{12,8},{16,20},{20,16},{24,28},{28,24},{32,36},... | collective-permute-start | bytes 3080 | tf_op jit(solution)/shard_map/ppermute | solution.py:11
  277.6 41.7 %while.10 = (s32[]{:T(128)}, f32[12,512,64]{1,2,0:T(8,128)}, pred[1,1024]{1,0:T(4,128)(4,1)S(1)}, bf16[12,512,64]{1,2,0:T(8,128)(2,1)}, bf16[12,1024,64]{1,2,0:T...) while((s32[]{:T(128)}, f32[12,512,64]{1,2,0:T(8,128)}, ...), condition=%wide.region_9.10_spmd, body=%wide.region_6.9_spmd.sunk | while | flops 141065216 | bytes 6767702 | solution.py:93
  319.2 3.6 reshape.533
  323.9 3.7 broadcast_select_fusion.1
  327.6 2.7 copy.135
  336.3 10.3 %collective-permute-done.11 = bf16[2,2,64,768]{3,2,1,0:T(8,128)(2,1)S(1)} collective-permute-done((bf16[2,2,64,768]{3,2,1,0:T(8,128)(2,1)S(1)}, bf16[2,2,64,768]{3,2,1,0:T(8,128)(2,1)S(1)}, u32[]{:S(2)}, u32[]{:S(2)}) %collective-permute-start.11) | collective-permute-done | bytes 393248 | tf_op jit(solution)/shard_map/ppermute | solution.py:11
  346.9 3.3 collective-permute-start.12
  350.3 18.8 %collective-permute-done.12 = bf16[1,4,64,768]{3,2,1,0:T(8,128)(2,1)S(1)} collective-permute-done((bf16[1,4,64,768]{3,2,1,0:T(8,128)(2,1)S(1)}, bf16[1,4,64,768]{3,2,1,0:T(8,128)(2,1)S(1)}, u32[]{:S(2)}, u32[]{:S(2)}) %collective-permute-start.12) | collective-permute-done | bytes 393248 | tf_op jit(solution)/shard_map/ppermute | solution.py:11
  369.3 2.7 gather_fusion.2
  (165 shorter events, 95.2 us)
Async XLA Ops:
  6.5 66.2 %copy-start = (bf16[256,768]{1,0:T(8,128)(2,1)S(1)}, bf16[256,768]{1,0:T(8,128)(2,1)}, u32[]{:S(2)}) copy-start(bf16[256,768]{1,0:T(8,128)(2,1)} %param.12) | copy-start | bytes 1179652
  6.5 28.7 %copy-start.3 = (bf16[32,64,256]{2,1,0:T(8,128)(2,1)S(1)}, bf16[32,64,256]{2,1,0:T(8,128)(2,1)}, u32[]{:S(2)}) copy-start(bf16[32,64,256]{2,1,0:T(8,128)(2,1)} %param.9) | copy-start | bytes 3145732
  6.5 66.2 %all-gather.4.cloned.1.call-start = ((), (), s32[]{:S(2)}) async-start(), calls=%async_computation | async-start | bytes 1474560 | tf_op jit(solution)/shard_map/all_gather | solution.py:119
  7.3 127.0 %all-gather.6.cloned.1.call-start = ((), (), s32[]{:S(2)}) async-start(), calls=%async_computation.1 | async-start | bytes 4755456 | tf_op jit(solution)/shard_map/all_gather | solution.py:139
  9.0 27.9 %collective-permute-start.4 = (bf16[32,1,256]{2,1,0:T(2,128)(2,1)S(1)}, bf16[32,1,256]{2,1,0:T(2,128)(2,1)S(1)}, u32[]{:S(2)}, u32[]{:S(2)}) collective-permute-start(bf16[32,1,256]{2,1,0:T(2,128)(2,1)S(1)} %slice.131), channel_id=1, source_target_pairs={{0,1},{1,2},{2,3},{4,5},{5,6},{6,7},{8,9},{9,10},{10,11},{12,13},{... | collective-permute-start | bytes 49160 | tf_op jit(solution)/shard_map/ppermute | solution.py:17
  36.9 15.6 %collective-permute-start.5 = (bf16[1,65,256]{2,1,0:T(8,128)(2,1)S(1)}, bf16[1,65,256]{2,1,0:T(8,128)(2,1)S(1)}, u32[]{:S(2)}, u32[]{:S(2)}) collective-permute-start(bf16[1,65,256]{2,1,0:T(8,128)(2,1)S(1)} %fusion.51), channel_id=1, source_target_pairs={{0,4},{4,8},{8,12},{12,16},{16,20},{20,24},{24,28},{28,32},{32,36}... | collective-permute-start | bytes 99848 | tf_op jit(solution)/shard_map/ppermute | solution.py:17
  53.2 15.0 %copy-start.7 = (bf16[16,32,256]{2,1,0:T(8,128)(2,1)S(1)}, bf16[16,32,256]{2,1,0:T(8,128)(2,1)}, u32[]{:S(2)}) copy-start(bf16[16,32,256]{2,1,0:T(8,128)(2,1)} %slice.136) | copy-start | bytes 786436
  58.3 10.7 %copy-start.5 = (bf16[16,32,256]{2,1,0:T(8,128)(2,1)S(1)}, bf16[16,32,256]{2,1,0:T(8,128)(2,1)}, u32[]{:S(2)}) copy-start(bf16[16,32,256]{2,1,0:T(8,128)(2,1)} %slice.137) | copy-start | bytes 786436
  63.9 6.6 %copy-start.6 = (bf16[16,32,256]{2,1,0:T(8,128)(2,1)S(1)}, bf16[16,32,256]{2,1,0:T(8,128)(2,1)}, u32[]{:S(2)}) copy-start(bf16[16,32,256]{2,1,0:T(8,128)(2,1)} %slice.139) | copy-start | bytes 786436
  68.2 4.6 %copy-start.9 = (f32[256]{0:T(256)S(1)}, f32[256]{0:T(256)}, u32[]{:S(2)}) copy-start(f32[256]{0:T(256)} %param.11) | copy-start | bytes 3076
  76.3 57.9 %copy-start.4 = (f32[512,768]{1,0:T(8,128)}, f32[512,768]{1,0:T(8,128)S(1)}, u32[]{:S(2)}) copy-start(f32[512,768]{1,0:T(8,128)S(1)} %get-tuple-element.113) | copy-start | bytes 4718596
  148.8 8.0 %copy-start.2 = (bf16[512,2304]{1,0:T(8,128)(2,1)S(1)}, bf16[512,2304]{1,0:T(8,128)(2,1)}, u32[]{:S(2)}) copy-start(bf16[512,2304]{1,0:T(8,128)(2,1)} %gather_fusion.1) | copy-start | bytes 7077892
  151.8 5.1 %collective-permute-start.6 = (bf16[4,1,64,2304]{3,2,0,1:T(8,128)(2,1)}, bf16[4,1,64,2304]{3,2,0,1:T(8,128)(2,1)}, u32[]{:S(2)}, u32[]{:S(2)}) collective-permute-start(bf16[4,1,64,2304]{3,2,0,1:T(8,128)(2,1)} %fusion.23), channel_id=1, source_target_pairs={{0,4},{4,0},{8,12},{12,8},{16,20},{20,16},{24,28},{28,24},{32,36},... | collective-permute-start | bytes 3538952 | tf_op jit(solution)/shard_map/ppermute | solution.py:11
  159.7 29.5 %collective-permute-start.7 = (bf16[2,2,64,2304]{3,2,1,0:T(8,128)(2,1)}, bf16[2,2,64,2304]{3,2,1,0:T(8,128)(2,1)}, u32[]{:S(2)}, u32[]{:S(2)}) collective-permute-start(bf16[2,2,64,2304]{3,2,1,0:T(8,128)(2,1)} %select_bitcast_fusion.1), channel_id=1, source_target_pairs={{0,8},{4,12},{8,0},{12,4},{16,24},{20,28},{24,16},{28,20},{32,40},... | collective-permute-start | bytes 3538952 | tf_op jit(solution)/shard_map/ppermute | solution.py:11
  190.9 4.5 %copy-start.8 = (s32[16,32]{1,0:T(8,128)S(1)}, s32[16,32]{1,0:T(8,128)}, u32[]{:S(2)}) copy-start(s32[16,32]{1,0:T(8,128)} %param.14) | copy-start | bytes 6148
  192.1 56.1 %collective-permute-start.8 = (bf16[1,4,64,2304]{3,2,1,0:T(8,128)(2,1)}, bf16[1,4,64,2304]{3,2,1,0:T(8,128)(2,1)}, u32[]{:S(2)}, u32[]{:S(2)}) collective-permute-start(bf16[1,4,64,2304]{3,2,1,0:T(8,128)(2,1)} %select_bitcast_fusion), channel_id=1, source_target_pairs={{0,16},{4,20},{8,24},{12,28},{16,0},{20,4},{24,8},{28,12},{32,48},... | collective-permute-start | bytes 3538952 | tf_op jit(solution)/shard_map/ppermute | solution.py:11
  251.3 21.8 %collective-permute-start.9 = (bf16[512,1536]{1,0:T(8,128)(2,1)}, bf16[512,1536]{1,0:T(8,128)(2,1)}, u32[]{:S(2)}, u32[]{:S(2)}) collective-permute-start(bf16[512,1536]{1,0:T(8,128)(2,1)} %slice.180), channel_id=1, source_target_pairs={{0,4},{4,0},{8,12},{12,8},{16,20},{20,16},{24,28},{28,24},{32,36},... | collective-permute-start | bytes 4718600 | tf_op jit(solution)/shard_map/ppermute | solution.py:11
  253.8 3.0 collective-permute-start
  256.9 4.3 %collective-permute-start.1 = (bf16[2,2,64]{2,1,0:T(2,128)(2,1)S(1)}, bf16[2,2,64]{2,1,0:T(2,128)(2,1)S(1)}, u32[]{:S(2)}, u32[]{:S(2)}) collective-permute-start(bf16[2,2,64]{2,1,0:T(2,128)(2,1)S(1)} %bitcast.242), channel_id=1, source_target_pairs={{0,8},{4,12},{8,0},{12,4},{16,24},{20,28},{24,16},{28,20},{32,40},... | collective-permute-start | bytes 1544 | tf_op jit(solution)/shard_map/ppermute | solution.py:11
  261.2 5.2 %collective-permute-start.2 = (bf16[1,4,64]{2,1,0:T(4,128)(2,1)S(1)}, bf16[1,4,64]{2,1,0:T(4,128)(2,1)S(1)}, u32[]{:S(2)}, u32[]{:S(2)}) collective-permute-start(bf16[1,4,64]{2,1,0:T(4,128)(2,1)S(1)} %select_bitcast_fusion.4), channel_id=1, source_target_pairs={{0,16},{4,20},{8,24},{12,28},{16,0},{20,4},{24,8},{28,12},{32,48},... | collective-permute-start | bytes 1544 | tf_op jit(solution)/shard_map/ppermute | solution.py:11
  266.6 5.3 %collective-permute-start.3 = (bf16[512]{0:T(512)(128)(2,1)S(1)}, bf16[512]{0:T(512)(128)(2,1)S(1)}, u32[]{:S(2)}, u32[]{:S(2)}) collective-permute-start(bf16[512]{0:T(512)(128)(2,1)S(1)} %reshape_reshape.30), channel_id=1, source_target_pairs={{0,4},{4,0},{8,12},{12,8},{16,20},{20,16},{24,28},{28,24},{32,36},... | collective-permute-start | bytes 3080 | tf_op jit(solution)/shard_map/ppermute | solution.py:11
  330.4 3.8 %collective-permute-start.10 = (bf16[4,1,64,768]{3,2,0,1:T(8,128)(2,1)}, bf16[4,1,64,768]{3,2,0,1:T(8,128)(2,1)S(1)}, u32[]{:S(2)}, u32[]{:S(2)}) collective-permute-start(bf16[4,1,64,768]{3,2,0,1:T(8,128)(2,1)} %bitcast.56), channel_id=1, source_target_pairs={{0,4},{4,0},{8,12},{12,8},{16,20},{20,16},{24,28},{28,24},{32,36},... | collective-permute-start | bytes 1179656 | tf_op jit(solution)/shard_map/ppermute | solution.py:11
  334.4 12.3 %collective-permute-start.11 = (bf16[2,2,64,768]{3,2,1,0:T(8,128)(2,1)S(1)}, bf16[2,2,64,768]{3,2,1,0:T(8,128)(2,1)S(1)}, u32[]{:S(2)}, u32[]{:S(2)}) collective-permute-start(bf16[2,2,64,768]{3,2,1,0:T(8,128)(2,1)S(1)} %select_bitcast_fusion.3), channel_id=1, source_target_pairs={{0,8},{4,12},{8,0},{12,4},{16,24},{20,28},{24,16},{28,20},{32,40},... | collective-permute-start | bytes 1179656 | tf_op jit(solution)/shard_map/ppermute | solution.py:11
  346.9 22.2 %collective-permute-start.12 = (bf16[1,4,64,768]{3,2,1,0:T(8,128)(2,1)S(1)}, bf16[1,4,64,768]{3,2,1,0:T(8,128)(2,1)S(1)}, u32[]{:S(2)}, u32[]{:S(2)}) collective-permute-start(bf16[1,4,64,768]{3,2,1,0:T(8,128)(2,1)S(1)} %select_bitcast_fusion.2), channel_id=1, source_target_pairs={{0,16},{4,20},{8,24},{12,28},{16,0},{20,4},{24,8},{28,12},{32,48},... | collective-permute-start | bytes 1179656 | tf_op jit(solution)/shard_map/ppermute | solution.py:11
  369.2 2.7 copy-start.1
Sparse Core Ops, SparseCore 0:
  9.5 34.2 all-gather.3
  46.9 87.2 all-gather.5
where the time goes:
time: 381 us; the launch traced here: 379 us
  waiting for transfers between devices  174 us (46%)
  local copies, waits for them, and re-layouts  81.4 us (21%)
  matrix products  41.6 us (11%)
  starting transfers between devices  38 us (10%)
  other arithmetic  29.8 us (8%)
  between operations  13.9 us (4%)
    ppermute x11, waiting for transfers between devices, partner(): lax.ppermute(array, axis, [(i, i ^ 1 << apart) for i in range(lax.axis_si...  115 us
    all_gather x1, waiting for transfers between devices, local(): lax.all_gather(qkv_weight, 'row', axis=0, tiled=True)  57.6 us
    slice x9, local copies, waits for them, and re-layouts, local(): padded[row_tap:row_tap + in_rows - 1:2, col_tap:col_tap + in_cols - 1:2, :]  38.1 us
    ppermute x11, starting transfers between devices, partner(): lax.ppermute(array, axis, [(i, i ^ 1 << apart) for i in range(lax.axis_si...  29.2 us
    dot_general x12, matrix products, one_head(): jnp.einsum('qd,kd->qk', query_head, key_head, preferred_element_type=jnp....  17.8 us
    dot_general x12, matrix products, one_head(): jnp.dot(weights.astype(jnp.bfloat16), value_head, preferred_element_type=...  15.8 us
    unnamed x30, local copies, waits for them, and re-layouts  14.7 us
    ppermute x2, starting transfers between devices, shifted(): return lax.ppermute(array, axis, pairs)  8.79 us
  transfers between devices with their start and end apart: 15, of which 11 were waited for; matrix products, arithmetic and copies ran while one was open for 17% of the time, Pallas kernels for 0%

commit v1 on v0

--- a/solution.py
+++ b/solution.py
@@ -136,9 +136,12 @@
     )
     tissue_flag = tissue.reshape(token_count).astype(jnp.bfloat16)
     flag_out = tissue_flag[inverse].reshape(owner_labels, capacity)
-    qkv_local = fold_rows(tokens_bf, lax.all_gather(qkv_weight, "row", axis=0, tiled=True)).astype(
-        jnp.bfloat16
-    )
+    qkv_local = fold_rows(
+        tokens_bf,
+        jnp.concatenate(
+            lax.all_to_all(jnp.stack([qkv_weight] * lax.axis_size("row")), "row", 0, 0), axis=0
+        ),
+    ).astype(jnp.bfloat16)
     arrived, arrived_flag = route_sender(
         qkv_local[inverse].reshape(owner_labels, capacity, 3 * model_width), flag_out
     )

time: 381 us -> 409 us (1.073)
  the two profiles are of different devices: /device:TPU:1 before, /device:TPU:63 now
where the time goes in v1:
time: 409 us; the launch traced here: 408 us
  waiting for transfers between devices  199 us (49%)
  local copies, waits for them, and re-layouts  73 us (18%)
  starting transfers between devices  50.6 us (12%)
  matrix products  41.6 us (10%)
  other arithmetic  29.1 us (7%)
  between operations  14 us (3%)
    ppermute x11, waiting for transfers between devices, partner(): lax.ppermute(array, axis, [(i, i ^ 1 << apart) for i in range(lax.axis_si...  117 us
    ppermute x2, waiting for transfers between devices, shifted(): return lax.ppermute(array, axis, pairs)  81.9 us
    slice x9, local copies, waits for them, and re-layouts, local(): padded[row_tap:row_tap + in_rows - 1:2, col_tap:col_tap + in_cols - 1:2, :]  28 us
    ppermute x11, starting transfers between devices, partner(): lax.ppermute(array, axis, [(i, i ^ 1 << apart) for i in range(lax.axis_si...  27.7 us
    all_to_all x1, starting transfers between devices, local(): lax.all_to_all(jnp.stack([qkv_weight] * lax.axis_size('row')), 'row', 0, 0)  18.2 us
    dot_general x12, matrix products, one_head(): jnp.einsum('qd,kd->qk', query_head, key_head, preferred_element_type=jnp....  17.8 us
    dot_general x12, matrix products, one_head(): jnp.dot(weights.astype(jnp.bfloat16), value_head, preferred_element_type=...  15.8 us
    unnamed x31, local copies, waits for them, and re-layouts  8.91 us
  transfers between devices with their start and end apart: 15, of which 11 were waited for; matrix products, arithmetic and copies ran while one was open for 13% of the time, Pallas kernels for 0%

profile of v1, /device:TPU:63, one launch (start us, length us, event | category | flops | bytes accessed | tf_op | source)
XLA Modules:
  0.0 407.6 jit_solution(6063986819426571524)
XLA Ops:
  6.5 3.3 stack.65
  9.8 18.2 %all-to-all-start = ((bf16[128,6,2304]{2,1,0:T(8,128)(2,1)}), bf16[128,6,2304]{2,1,0:T(8,128)(2,1)}, u32[]{:S(2)}, u32[]{:S(2)}) async-start(bf16[128,6,2304]{2,1,0:T(8,128)(2,1)} %stack.65), calls=%async_computation | async-start | bytes 9437184 | tf_op jit(solution)/shard_map/all_to_all | solution.py:142
  31.5 2.4 scatter_custom_fusion
  33.9 5.1 %slice.137 = bf16[16,32,256]{2,1,0:T(8,128)(2,1)} slice(bf16[32,64,256]{2,1,0:T(8,128)(2,1)S(1)} %copy-done.3), slice={[0:31:2], [0:63:2], [0:256:1]} | slice | bytes 524288 | tf_op jit(solution)/shard_map/slice | solution.py:114
  41.2 3.4 collective-permute-start.5
  45.2 5.0 %slice.136 = bf16[16,32,256]{2,1,0:T(8,128)(2,1)} slice(bf16[32,65,256]{2,1,0:T(8,128)(2,1)S(1)} %pad_maximum_fusion.2), slice={[0:31:2], [0:63:2], [0:256:1]} | slice | bytes 524288 | tf_op jit(solution)/shard_map/slice | solution.py:114
  50.2 5.0 %slice.139 = bf16[16,32,256]{2,1,0:T(8,128)(2,1)} slice(bf16[32,65,256]{2,1,0:T(8,128)(2,1)S(1)} %pad_maximum_fusion.2), slice={[1:32:2], [0:63:2], [0:256:1]} | slice | bytes 524288 | tf_op jit(solution)/shard_map/slice | solution.py:114
  55.3 81.9 %collective-permute-done.5 = bf16[1,65,256]{2,1,0:T(8,128)(2,1)S(1)} collective-permute-done((bf16[1,65,256]{2,1,0:T(8,128)(2,1)S(1)}, bf16[1,65,256]{2,1,0:T(8,128)(2,1)S(1)}, u32[]{:S(2)}, u32[]{:S(2)}) %collective-permute-start.5) | collective-permute-done | bytes 33312 | tf_op jit(solution)/shard_map/ppermute | solution.py:17
  137.9 5.1 %slice.133 = bf16[16,32,256]{2,1,0:T(8,128)(2,1)} slice(bf16[33,65,256]{2,1,0:T(8,128)(2,1)S(1)} %maximum_maximum_fusion), slice={[0:31:2], [0:63:2], [0:256:1]} | slice | bytes 524288 | tf_op jit(solution)/shard_map/slice | solution.py:114
  142.9 5.0 %slice.134 = bf16[16,32,256]{2,1,0:T(8,128)(2,1)} slice(bf16[33,65,256]{2,1,0:T(8,128)(2,1)S(1)} %maximum_maximum_fusion), slice={[0:31:2], [1:64:2], [0:256:1]} | slice | bytes 524288 | tf_op jit(solution)/shard_map/slice | solution.py:114
  157.4 3.5 fusion.67
  162.1 6.6 %reshape.535 = bf16[768,2304]{1,0:T(8,128)(2,1)} reshape(bf16[128,6,2304]{2,1,0:T(8,128)(2,1)} %all-to-all-done) | data formatting | bytes 7077888 | tf_op jit(solution)/shard_map/reshape | solution.py:141
  168.7 4.5 %convolution_convert_fusion = bf16[512,2304]{1,0:T(8,128)(2,1)S(1)} fusion(bf16[768,2304]{1,0:T(8,128)(2,1)} %reshape.535, f32[512,768]{1,0:T(8,128)} %copy-done.4, f32[512]{0:T(512)S(1)} %add_rsqrt_fusion, f32[512]{0:T(512)S(1)} %broadcast_multiply_fusion.1), kind=kOutput, calls=%fused_computation.28 | convolution fusion | flops 1814298624 | bytes 7475200 | tf_op jit(solution)/shard_map/dot_general | solution.py:27
  173.2 3.4 gather_fusion.1
  176.6 2.9 fusion.23
  181.5 3.1 collective-permute-done.6
  187.5 4.1 %collective-permute-start.7 = (bf16[2,2,64,2304]{3,2,1,0:T(8,128)(2,1)}, bf16[2,2,64,2304]{3,2,1,0:T(8,128)(2,1)}, u32[]{:S(2)}, u32[]{:S(2)}) collective-permute-start(bf16[2,2,64,2304]{3,2,1,0:T(8,128)(2,1)} %select_bitcast_fusion.1), channel_id=1, source_target_pairs={{0,8},{4,12},{8,0},{12,4},{16,24},{20,28},{24,16},{28,20},{32,40},... | collective-permute-start | bytes 3538952 | tf_op jit(solution)/shard_map/ppermute | solution.py:11
  191.6 26.3 %collective-permute-done.7 = bf16[2,2,64,2304]{3,2,1,0:T(8,128)(2,1)} collective-permute-done((bf16[2,2,64,2304]{3,2,1,0:T(8,128)(2,1)}, bf16[2,2,64,2304]{3,2,1,0:T(8,128)(2,1)}, u32[]{:S(2)}, u32[]{:S(2)}) %collective-permute-start.7) | collective-permute-done | bytes 1179680 | tf_op jit(solution)/shard_map/ppermute | solution.py:11
  223.1 3.5 gather_fusion
  226.7 49.6 %collective-permute-done.8 = bf16[1,4,64,2304]{3,2,1,0:T(8,128)(2,1)} collective-permute-done((bf16[1,4,64,2304]{3,2,1,0:T(8,128)(2,1)}, bf16[1,4,64,2304]{3,2,1,0:T(8,128)(2,1)}, u32[]{:S(2)}, u32[]{:S(2)}) %collective-permute-start.8) | collective-permute-done | bytes 1179680 | tf_op jit(solution)/shard_map/ppermute | solution.py:11
  279.2 3.3 collective-permute-start.9
  287.5 2.4 collective-permute-done.1
  291.9 3.3 collective-permute-done.2
  295.3 4.5 %collective-permute-start.3 = (bf16[512]{0:T(512)(128)(2,1)S(1)}, bf16[512]{0:T(512)(128)(2,1)S(1)}, u32[]{:S(2)}, u32[]{:S(2)}) collective-permute-start(bf16[512]{0:T(512)(128)(2,1)S(1)} %reshape_reshape.30), channel_id=1, source_target_pairs={{0,4},{4,0},{8,12},{12,8},{16,20},{20,16},{24,28},{28,24},{32,36},... | collective-permute-start | bytes 3080 | tf_op jit(solution)/shard_map/ppermute | solution.py:11
  306.3 41.7 %while.10 = (s32[]{:T(128)}, f32[12,512,64]{1,2,0:T(8,128)}, pred[1,1024]{1,0:T(4,128)(4,1)S(1)}, bf16[12,512,64]{1,2,0:T(8,128)(2,1)}, bf16[12,1024,64]{1,2,0:T...) while((s32[]{:T(128)}, f32[12,512,64]{1,2,0:T(8,128)}, ...), condition=%wide.region_9.10_spmd, body=%wide.region_6.9_spmd.sunk | while | flops 141065216 | bytes 6767702 | solution.py:93
  348.0 3.6 reshape.539
  352.7 3.7 broadcast_select_fusion.1
  356.4 2.7 copy.114
  359.1 2.2 collective-permute-start.10
  365.0 10.3 %collective-permute-done.11 = bf16[2,2,64,768]{3,2,1,0:T(8,128)(2,1)S(1)} collective-permute-done((bf16[2,2,64,768]{3,2,1,0:T(8,128)(2,1)S(1)}, bf16[2,2,64,768]{3,2,1,0:T(8,128)(2,1)S(1)}, u32[]{:S(2)}, u32[]{:S(2)}) %collective-permute-start.11) | collective-permute-done | bytes 393248 | tf_op jit(solution)/shard_map/ppermute | solution.py:11
  377.6 20.3 %collective-permute-done.12 = bf16[1,4,64,768]{3,2,1,0:T(8,128)(2,1)S(1)} collective-permute-done((bf16[1,4,64,768]{3,2,1,0:T(8,128)(2,1)S(1)}, bf16[1,4,64,768]{3,2,1,0:T(8,128)(2,1)S(1)}, u32[]{:S(2)}, u32[]{:S(2)}) %collective-permute-start.12) | collective-permute-done | bytes 393248 | tf_op jit(solution)/shard_map/ppermute | solution.py:11
  398.0 2.7 gather_fusion.2
  (167 shorter events, 92.5 us)
Async XLA Ops:
  6.5 150.9 %copy-start = (bf16[256,768]{1,0:T(8,128)(2,1)S(1)}, bf16[256,768]{1,0:T(8,128)(2,1)}, u32[]{:S(2)}) copy-start(bf16[256,768]{1,0:T(8,128)(2,1)} %param.12) | copy-start | bytes 1179652
  9.8 18.2 %copy-start.3 = (bf16[32,64,256]{2,1,0:T(8,128)(2,1)S(1)}, bf16[32,64,256]{2,1,0:T(8,128)(2,1)}, u32[]{:S(2)}) copy-start(bf16[32,64,256]{2,1,0:T(8,128)(2,1)} %param.9) | copy-start | bytes 3145732
  9.8 19.6 %copy-start.8 = (s32[16,32]{1,0:T(8,128)S(1)}, s32[16,32]{1,0:T(8,128)}, u32[]{:S(2)}) copy-start(s32[16,32]{1,0:T(8,128)} %param.15) | copy-start | bytes 6148
  9.8 151.4 %all-to-all-start = ((bf16[128,6,2304]{2,1,0:T(8,128)(2,1)}), bf16[128,6,2304]{2,1,0:T(8,128)(2,1)}, u32[]{:S(2)}, u32[]{:S(2)}) async-start(bf16[128,6,2304]{2,1,0:T(8,128)(2,1)} %stack.65), calls=%async_computation | async-start | bytes 9437184 | tf_op jit(solution)/shard_map/all_to_all | solution.py:142
  28.0 129.4 %all-gather.2.cloned.1.call-start = ((), (), s32[]{:S(2)}) async-start(), calls=%async_computation.1 | async-start | bytes 1474560 | tf_op jit(solution)/shard_map/all_gather | solution.py:119
  28.1 13.0 %collective-permute-start.4 = (bf16[32,1,256]{2,1,0:T(2,128)(2,1)S(1)}, bf16[32,1,256]{2,1,0:T(2,128)(2,1)S(1)}, u32[]{:S(2)}, u32[]{:S(2)}) collective-permute-start(bf16[32,1,256]{2,1,0:T(2,128)(2,1)S(1)} %slice.131), channel_id=1, source_target_pairs={{0,1},{1,2},{2,3},{4,5},{5,6},{6,7},{8,9},{9,10},{10,11},{12,13},{... | collective-permute-start | bytes 49160 | tf_op jit(solution)/shard_map/ppermute | solution.py:17
  41.2 96.0 %collective-permute-start.5 = (bf16[1,65,256]{2,1,0:T(8,128)(2,1)S(1)}, bf16[1,65,256]{2,1,0:T(8,128)(2,1)S(1)}, u32[]{:S(2)}, u32[]{:S(2)}) collective-permute-start(bf16[1,65,256]{2,1,0:T(8,128)(2,1)S(1)} %fusion.51), channel_id=1, source_target_pairs={{0,4},{4,8},{8,12},{12,16},{16,20},{20,24},{24,28},{28,32},{32,36}... | collective-permute-start | bytes 99848 | tf_op jit(solution)/shard_map/ppermute | solution.py:17
  137.8 15.0 %copy-start.7 = (bf16[16,32,256]{2,1,0:T(8,128)(2,1)S(1)}, bf16[16,32,256]{2,1,0:T(8,128)(2,1)}, u32[]{:S(2)}) copy-start(bf16[16,32,256]{2,1,0:T(8,128)(2,1)} %slice.136) | copy-start | bytes 786436
  142.9 10.7 %copy-start.5 = (bf16[16,32,256]{2,1,0:T(8,128)(2,1)S(1)}, bf16[16,32,256]{2,1,0:T(8,128)(2,1)}, u32[]{:S(2)}) copy-start(bf16[16,32,256]{2,1,0:T(8,128)(2,1)} %slice.137) | copy-start | bytes 786436
  148.6 6.5 %copy-start.6 = (bf16[16,32,256]{2,1,0:T(8,128)(2,1)S(1)}, bf16[16,32,256]{2,1,0:T(8,128)(2,1)}, u32[]{:S(2)}) copy-start(bf16[16,32,256]{2,1,0:T(8,128)(2,1)} %slice.139) | copy-start | bytes 786436
  152.9 4.5 %copy-start.10 = (f32[256]{0:T(256)S(1)}, f32[256]{0:T(256)}, u32[]{:S(2)}) copy-start(f32[256]{0:T(256)} %param.11) | copy-start | bytes 3076
  160.9 1.2 copy-start.4
  176.6 8.0 %copy-start.2 = (bf16[512,2304]{1,0:T(8,128)(2,1)S(1)}, bf16[512,2304]{1,0:T(8,128)(2,1)}, u32[]{:S(2)}) copy-start(bf16[512,2304]{1,0:T(8,128)(2,1)} %gather_fusion.1) | copy-start | bytes 7077892
  179.6 5.1 %collective-permute-start.6 = (bf16[4,1,64,2304]{3,2,0,1:T(8,128)(2,1)}, bf16[4,1,64,2304]{3,2,0,1:T(8,128)(2,1)}, u32[]{:S(2)}, u32[]{:S(2)}) collective-permute-start(bf16[4,1,64,2304]{3,2,0,1:T(8,128)(2,1)} %fusion.23), channel_id=1, source_target_pairs={{0,4},{4,0},{8,12},{12,8},{16,20},{20,16},{24,28},{28,24},{32,36},... | collective-permute-start | bytes 3538952 | tf_op jit(solution)/shard_map/ppermute | solution.py:11
  187.5 30.4 %collective-permute-start.7 = (bf16[2,2,64,2304]{3,2,1,0:T(8,128)(2,1)}, bf16[2,2,64,2304]{3,2,1,0:T(8,128)(2,1)}, u32[]{:S(2)}, u32[]{:S(2)}) collective-permute-start(bf16[2,2,64,2304]{3,2,1,0:T(8,128)(2,1)} %select_bitcast_fusion.1), channel_id=1, source_target_pairs={{0,8},{4,12},{8,0},{12,4},{16,24},{20,28},{24,16},{28,20},{32,40},... | collective-permute-start | bytes 3538952 | tf_op jit(solution)/shard_map/ppermute | solution.py:11
  219.7 3.3 copy-start.9
  220.9 55.4 %collective-permute-start.8 = (bf16[1,4,64,2304]{3,2,1,0:T(8,128)(2,1)}, bf16[1,4,64,2304]{3,2,1,0:T(8,128)(2,1)}, u32[]{:S(2)}, u32[]{:S(2)}) collective-permute-start(bf16[1,4,64,2304]{3,2,1,0:T(8,128)(2,1)} %select_bitcast_fusion), channel_id=1, source_target_pairs={{0,16},{4,20},{8,24},{12,28},{16,0},{20,4},{24,8},{28,12},{32,48},... | collective-permute-start | bytes 3538952 | tf_op jit(solution)/shard_map/ppermute | solution.py:11
  279.2 22.6 %collective-permute-start.9 = (bf16[512,1536]{1,0:T(8,128)(2,1)}, bf16[512,1536]{1,0:T(8,128)(2,1)}, u32[]{:S(2)}, u32[]{:S(2)}) collective-permute-start(bf16[512,1536]{1,0:T(8,128)(2,1)} %slice.180), channel_id=1, source_target_pairs={{0,4},{4,0},{8,12},{12,8},{16,20},{20,16},{24,28},{28,24},{32,36},... | collective-permute-start | bytes 4718600 | tf_op jit(solution)/shard_map/ppermute | solution.py:11
  282.6 3.0 collective-permute-start
  285.6 4.3 %collective-permute-start.1 = (bf16[2,2,64]{2,1,0:T(2,128)(2,1)S(1)}, bf16[2,2,64]{2,1,0:T(2,128)(2,1)S(1)}, u32[]{:S(2)}, u32[]{:S(2)}) collective-permute-start(bf16[2,2,64]{2,1,0:T(2,128)(2,1)S(1)} %bitcast.240), channel_id=1, source_target_pairs={{0,8},{4,12},{8,0},{12,4},{16,24},{20,28},{24,16},{28,20},{32,40},... | collective-permute-start | bytes 1544 | tf_op jit(solution)/shard_map/ppermute | solution.py:11
  290.0 5.2 %collective-permute-start.2 = (bf16[1,4,64]{2,1,0:T(4,128)(2,1)S(1)}, bf16[1,4,64]{2,1,0:T(4,128)(2,1)S(1)}, u32[]{:S(2)}, u32[]{:S(2)}) collective-permute-start(bf16[1,4,64]{2,1,0:T(4,128)(2,1)S(1)} %select_bitcast_fusion.4), channel_id=1, source_target_pairs={{0,16},{4,20},{8,24},{12,28},{16,0},{20,4},{24,8},{28,12},{32,48},... | collective-permute-start | bytes 1544 | tf_op jit(solution)/shard_map/ppermute | solution.py:11
  295.3 5.3 %collective-permute-start.3 = (bf16[512]{0:T(512)(128)(2,1)S(1)}, bf16[512]{0:T(512)(128)(2,1)S(1)}, u32[]{:S(2)}, u32[]{:S(2)}) collective-permute-start(bf16[512]{0:T(512)(128)(2,1)S(1)} %reshape_reshape.30), channel_id=1, source_target_pairs={{0,4},{4,0},{8,12},{12,8},{16,20},{20,16},{24,28},{28,24},{32,36},... | collective-permute-start | bytes 3080 | tf_op jit(solution)/shard_map/ppermute | solution.py:11
  359.1 3.8 collective-permute-start.10
  363.1 12.3 %collective-permute-start.11 = (bf16[2,2,64,768]{3,2,1,0:T(8,128)(2,1)S(1)}, bf16[2,2,64,768]{3,2,1,0:T(8,128)(2,1)S(1)}, u32[]{:S(2)}, u32[]{:S(2)}) collective-permute-start(bf16[2,2,64,768]{3,2,1,0:T(8,128)(2,1)S(1)} %select_bitcast_fusion.3), channel_id=1, source_target_pairs={{0,8},{4,12},{8,0},{12,4},{16,24},{20,28},{24,16},{28,20},{32,40},... | collective-permute-start | bytes 1179656 | tf_op jit(solution)/shard_map/ppermute | solution.py:11
  375.7 22.2 %collective-permute-start.12 = (bf16[1,4,64,768]{3,2,1,0:T(8,128)(2,1)S(1)}, bf16[1,4,64,768]{3,2,1,0:T(8,128)(2,1)S(1)}, u32[]{:S(2)}, u32[]{:S(2)}) collective-permute-start(bf16[1,4,64,768]{3,2,1,0:T(8,128)(2,1)S(1)} %select_bitcast_fusion.2), channel_id=1, source_target_pairs={{0,16},{4,20},{8,24},{12,28},{16,0},{20,4},{24,8},{28,12},{32,48},... | collective-permute-start | bytes 1179656 | tf_op jit(solution)/shard_map/ppermute | solution.py:11
  398.0 2.7 copy-start.1
Sparse Core Ops, SparseCore 0:
  31.0 28.2 all-gather.1
